TPU v7x, 256 devices: a whole 4x4x8 slice. The times are simulated.
256 devices in a mesh: mp: 32 (over z, y_hi, core), dp: 8 (over x, y_lo).
Axes of the slice: x: 4, y: 4 (y_hi: 2, y_lo: 2; y = y_hi * 2 + y_lo), z: 8, core: 2. Of those that a mesh axis runs over, the one named last changes fastest.
Arguments:
- tokens: bfloat16 [1024, 8192], P('mp', 'dp'), may hold values from -6 to 6
- gate_weight: bfloat16 [8192, 16384], P('dp', 'mp'), may hold values from -0.0625 to 0.0625
- up_weight: bfloat16 [8192, 16384], P('dp', 'mp'), may hold values from -0.0625 to 0.0625
- down_weight: bfloat16 [16384, 8192], P('mp', 'dp'), may hold values from -0.046875 to 0.046875
- cotangent: bfloat16 [1024, 8192], P('mp', 'dp'), may hold values from -6 to 6
Outputs:
- mixed: bfloat16 [1024, 8192], P('mp', 'dp')
- token_grad: bfloat16 [1024, 8192], P('mp', 'dp')
- gate_grad: bfloat16 [8192, 16384], P('dp', 'mp')
- up_grad: bfloat16 [8192, 16384], P('dp', 'mp')
- down_grad: bfloat16 [16384, 8192], P('mp', 'dp')
All inputs are finite; a program needn't handle non-finite values.
Results may differ from a plain program's by a relative error of at most 0.005.
Values may be sent and summed in bfloat16 or wider, within the bound.
No kernel may reach another device: no remote copies, remote signals or barrier semaphores. Data moves between devices by JAX's collectives and lax.ppermute only.
A program may use at most 64 MiB of HBM per device.

v0:
```python
import jax
import jax.numpy as jnp
from jax import lax
from jax.sharding import PartitionSpec as P


def contract_rows(left, right):
    return lax.dot_general(
        left, right, (((0,), (0,)), ((), ())), preferred_element_type=jnp.float32
    )


def contract_cols(left, right):
    return lax.dot_general(
        left, right, (((1,), (1,)), ((), ())), preferred_element_type=jnp.float32
    )


def body(tokens, gate_weight, up_weight, down_weight, cotangent):
    token_all = lax.all_gather(tokens, "mp", axis=0, tiled=True)
    width = gate_weight.shape[1]
    block = token_all
    first = jnp.dot(block, gate_weight, preferred_element_type=jnp.float32)
    second = jnp.dot(block, up_weight, preferred_element_type=jnp.float32)
    both = lax.psum(jnp.concatenate([first, second], axis=1), "dp")
    gate = both[:, :width]
    up = both[:, width:]
    sig = jax.nn.sigmoid(gate)
    act = gate * sig
    hidden_part = (act * up).astype(jnp.bfloat16)
    block = hidden_part
    mixed = lax.psum_scatter(
        jnp.dot(block, down_weight, preferred_element_type=jnp.float32),
        "mp",
        scatter_dimension=0,
        tiled=True,
    ).astype(jnp.bfloat16)
    cot_all = lax.all_gather(cotangent, "mp", axis=0, tiled=True)
    down_grad = contract_rows(hidden_part, cot_all).astype(jnp.bfloat16)
    block = cot_all
    hidden_back = lax.psum(contract_cols(block, down_weight), "dp")
    pre_gate = (hidden_back * up * sig * (1.0 + gate * (1.0 - sig))).astype(jnp.bfloat16)
    pre_up = (hidden_back * act).astype(jnp.bfloat16)
    gate_all, up_all = (pre_gate, pre_up)
    gate_grad = contract_rows(token_all, gate_all).astype(jnp.bfloat16)
    up_grad = contract_rows(token_all, up_all).astype(jnp.bfloat16)
    first = gate_all
    second = up_all
    token_grad = lax.psum_scatter(
        contract_cols(first, gate_weight) + contract_cols(second, up_weight),
        "mp",
        scatter_dimension=0,
        tiled=True,
    ).astype(jnp.bfloat16)
    return (mixed, token_grad, gate_grad, up_grad, down_grad)


def solution(mesh):
    in_specs = (P("mp", "dp"), P("dp", "mp"), P("dp", "mp"), P("mp", "dp"), P("mp", "dp"))
    out_specs = (P("mp", "dp"), P("mp", "dp"), P("dp", "mp"), P("dp", "mp"), P("mp", "dp"))
    return jax.shard_map(body, mesh=mesh, in_specs=in_specs, out_specs=out_specs, check_vma=False)
```

profile of v0, /device:TPU:6, one launch (start us, length us, event | category | flops | bytes accessed | tf_op | source)
XLA Modules:
  0.0 717.8 jit_solution(3119205423730051404)
XLA Ops:
  7.2 0.7 all-gather.3.cloned.1.call-update
  8.0 0.7 all-gather.5.cloned.1.call-update
  8.7 84.9 %all-gather.3.cloned.1.call-done = bf16[1024,1024]{1,0:T(8,128)(2,1)} async-done(((bf16[32,1024]{1,0:T(8,128)(2,1)}), bf16[1024,1024]{1,0:T(8,128)(2,1)}) %all-gather.3.cloned.1.call-update) | async-done | bytes 2097168 | tf_op jit(solution)/shard_map/all_gather | solution.py:20
  93.6 3.3 fusion.4
  96.9 1.3 fusion.3
  98.2 2.5 pad_maximum_fusion
  100.7 72.0 %all-gather.5.cloned.1.call-done = bf16[1024,1024]{1,0:T(8,128)(2,1)} async-done(((bf16[32,1024]{1,0:T(8,128)(2,1)}), bf16[1024,1024]{1,0:T(8,128)(2,1)}) %all-gather.5.cloned.1.call-update) | async-done | bytes 2097168 | tf_op jit(solution)/shard_map/all_gather | solution.py:38
  172.7 4.2 fusion.6
  177.0 262.9 %all-reduce.3.cloned.1.call-done = (f32[1024,1024]{0,1:T(8,128)}, f32[1024,512]{0,1:T(8,128)}) async-done(((f32[1024,1024]{0,1:T(8,128)}, f32[1024,512]{0,1:T(8,128)}), (f32[1024,1024]{0,1:T(8,128)}, f32[1024,512]{0,1:T(8,128)})) %all-reduce.3.cloned.1.call-update) | async-done | bytes 6291472 | tf_op jit(solution)/shard_map/psum | solution.py:25
  439.9 4.3 multiply_convert_fusion
  444.2 1.3 fusion.7
  445.5 0.3 copy-done.1
  445.8 3.3 convolution_add_fusion
  449.1 0.2 reduce-scatter.3.cloned.1.call-start
  449.3 4.5 fusion.5
  453.8 4.1 fusion.1
  458.0 2.3 copy.11
  460.3 3.8 fusion.2
  464.1 2.3 copy.12
  466.4 3.9 convolution_convert_fusion
  470.2 109.2 %reduce-scatter.5.cloned.1.call-done = f32[32,1024]{1,0:T(8,128)} async-done(((f32[1024,1024]{1,0:T(8,128)}), f32[32,1024]{1,0:T(8,128)}) %reduce-scatter.5.cloned.1.call-update) | async-done | bytes 131088 | tf_op jit(solution)/shard_map/reduce_scatter | solution.py:49
  579.4 1.5 convert_element_type.34
  581.0 128.8 %reduce-scatter.3.cloned.1.call-done = f32[32,1024]{1,0:T(8,128)} async-done(((f32[1024,1024]{1,0:T(8,128)}), f32[32,1024]{1,0:T(8,128)}) %reduce-scatter.3.cloned.1.call-update) | async-done | bytes 131088 | tf_op jit(solution)/shard_map/reduce_scatter | solution.py:32
  709.8 1.5 convert_element_type.31
  (16 shorter events, 0.2 us)
Async XLA Ops:
  7.2 89.7 %copy-start = (bf16[1024,512]{1,0:T(8,128)(2,1)S(1)}, bf16[1024,512]{1,0:T(8,128)(2,1)}, u32[]{:S(2)}) copy-start(bf16[1024,512]{1,0:T(8,128)(2,1)} %param.6) | copy-start | bytes 3145732
  7.2 86.4 %all-gather.3.cloned.1.call-start = ((), (), s32[]{:S(2)}) async-start(), calls=%async_computation.2 | async-start | bytes 2162688 | tf_op jit(solution)/shard_map/all_gather | solution.py:20
  7.9 164.8 %all-gather.5.cloned.1.call-start = ((), (), s32[]{:S(2)}) async-start(), calls=%async_computation.4 | async-start | bytes 2162688 | tf_op jit(solution)/shard_map/all_gather | solution.py:38
  8.7 431.2 %all-reduce.3.cloned.1.call-start = ((), (), s32[]{:S(2)}) async-start(), calls=%async_computation.6 | async-start | bytes 12582912 | tf_op jit(solution)/shard_map/psum | solution.py:25
  93.6 3.3 copy-start.4
  98.2 74.5 %copy-start.3 = (bf16[512,1024]{1,0:T(8,128)(2,1)S(1)}, bf16[512,1024]{1,0:T(8,128)(2,1)}, u32[]{:S(2)}) copy-start(bf16[512,1024]{1,0:T(8,128)(2,1)} %param.8) | copy-start | bytes 3145732
  176.9 402.5 %reduce-scatter.5.cloned.1.call-start = ((), (), s32[]{:S(2)}) async-start(), calls=%async_computation.5 | async-start | bytes 4325376 | tf_op jit(solution)/shard_map/reduce_scatter | solution.py:49
  444.2 1.3 copy-start.2
  444.2 1.6 copy-start.1
  449.1 260.7 %reduce-scatter.3.cloned.1.call-start = ((), (), s32[]{:S(2)}) async-start(), calls=%async_computation.3 | async-start | bytes 4325376 | tf_op jit(solution)/shard_map/reduce_scatter | solution.py:32
Sparse Core Ops, SparseCore 0:
  10.8 82.7 all-gather.2
  96.4 76.3 all-gather.4
  177.1 262.8 all-reduce.2
  449.2 130.1 reduce-scatter.4
  583.5 126.2 reduce-scatter.2
where the time goes:
time: 718 us
  waiting for transfers between devices  659 us (92%)
  matrix products  29.7 us (4%)
  between operations  13.9 us (2%)
  other arithmetic  9.84 us (1%)
    psum x1, waiting for transfers between devices, body(): both = lax.psum(jnp.concatenate([first, second], axis=1), 'dp')  263 us
    reduce_scatter x1, waiting for transfers between devices, body(): lax.psum_scatter(jnp.dot(block, down_weight, preferred_element_type=jnp.f...  129 us
    reduce_scatter x1, waiting for transfers between devices, body(): lax.psum_scatter(contract_cols(first, gate_weight) + contract_cols(second...  109 us
    all_gather x1, waiting for transfers between devices, body(): token_all = lax.all_gather(tokens, 'mp', axis=0, tiled=True)  84.9 us
    all_gather x1, waiting for transfers between devices, body(): cot_all = lax.all_gather(cotangent, 'mp', axis=0, tiled=True)  72 us
  transfers between devices with their start and end apart: 5, of which 5 were waited for; matrix products, arithmetic and copies ran while one was open for 4% of the time, Pallas kernels for 0%

commit v1 on v0

--- a/solution.py
+++ b/solution.py
@@ -35,7 +35,9 @@
         scatter_dimension=0,
         tiled=True,
     ).astype(jnp.bfloat16)
-    cot_all = lax.all_gather(cotangent, "mp", axis=0, tiled=True)
+    cot_all = jnp.concatenate(
+        lax.all_to_all(jnp.stack([cotangent] * lax.axis_size("mp")), "mp", 0, 0), axis=0
+    )
     down_grad = contract_rows(hidden_part, cot_all).astype(jnp.bfloat16)
     block = cot_all
     hidden_back = lax.psum(contract_cols(block, down_weight), "dp")

time: 718 us -> 652 us (0.908)
  waiting for transfers between devices: 659 us -> 579 us
  starting transfers between devices: 0.38 us -> 11.8 us
    all_gather x1 -> x0, waiting for transfers between devices: 72 us -> none  [body(): cot_all = lax.all_gather(cotangent, 'mp', axis=0, tiled=True)]
    all_to_all x0 -> x1, starting transfers between devices: none -> 11.5 us  [body(): lax.all_to_all(jnp.stack([cotangent] * lax.axis_size('mp')), 'mp', 0, 0)]
    all_gather x1, waiting for transfers between devices: 84.9 us -> 76.9 us  [body(): token_all = lax.all_gather(tokens, 'mp', axis=0, tiled=True)]
  transfers between devices with their start and end apart: 5 -> 5, of which waited for: 5 -> 4; matrix products, arithmetic and copies ran while one was open for 4% -> 5% of each run, Pallas kernels for 0% -> 0%
where the time goes in v1:
time: 652 us; the launch traced here: 651 us
  waiting for transfers between devices  579 us (89%)
  matrix products  30.1 us (5%)
  between operations  13.9 us (2%)
  starting transfers between devices  11.8 us (2%)
  other arithmetic  9.81 us (2%)
  local copies, waits for them, and re-layouts  7.29 us (1%)
    psum x1, waiting for transfers between devices, body(): both = lax.psum(jnp.concatenate([first, second], axis=1), 'dp')  263 us
    reduce_scatter x1, waiting for transfers between devices, body(): lax.psum_scatter(jnp.dot(block, down_weight, preferred_element_type=jnp.f...  129 us
    reduce_scatter x1, waiting for transfers between devices, body(): lax.psum_scatter(contract_cols(first, gate_weight) + contract_cols(second...  109 us
    all_gather x1, waiting for transfers between devices, body(): token_all = lax.all_gather(tokens, 'mp', axis=0, tiled=True)  76.9 us
  transfers between devices with their start and end apart: 5, of which 4 were waited for; matrix products, arithmetic and copies ran while one was open for 5% of the time, Pallas kernels for 0%

profile of v1, /device:TPU:6, one launch (start us, length us, event | category | flops | bytes accessed | tf_op | source)
XLA Modules:
  0.0 651.4 jit_solution(13296313691385874103)
XLA Ops:
  7.2 0.7 all-gather.2.cloned.1.call-update
  7.9 2.4 stack.2
  10.4 11.5 %all-to-all-start = ((bf16[32,32,1024]{2,1,0:T(8,128)(2,1)}), bf16[32,32,1024]{2,1,0:T(8,128)(2,1)S(1)}, u32[]{:S(2)}, u32[]{:S(2)}) async-start(bf16[32,32,1024]{2,1,0:T(8,128)(2,1)} %stack.2), calls=%async_computation.1 | async-start | bytes 4194304 | tf_op jit(solution)/shard_map/all_to_all | solution.py:39
  21.9 76.9 %all-gather.2.cloned.1.call-done = bf16[1024,1024]{1,0:T(8,128)(2,1)} async-done(((bf16[32,1024]{1,0:T(8,128)(2,1)}), bf16[1024,1024]{1,0:T(8,128)(2,1)}) %all-gather.2.cloned.1.call-update) | async-done | bytes 2097168 | tf_op jit(solution)/shard_map/all_gather | solution.py:20
  98.8 3.3 fusion.4
  102.1 1.3 fusion.3
  103.5 2.5 pad_maximum_fusion
  105.9 4.6 fusion.6
  110.6 262.9 %all-reduce.3.cloned.1.call-done = (f32[1024,1024]{0,1:T(8,128)}, f32[1024,512]{0,1:T(8,128)}) async-done(((f32[1024,1024]{0,1:T(8,128)}, f32[1024,512]{0,1:T(8,128)}), (f32[1024,1024]{0,1:T(8,128)}, f32[1024,512]{0,1:T(8,128)})) %all-reduce.3.cloned.1.call-update) | async-done | bytes 6291472 | tf_op jit(solution)/shard_map/psum | solution.py:25
  373.5 4.3 multiply_convert_fusion
  377.8 1.3 fusion.7
  379.1 0.3 copy-done.2
  379.4 3.3 convolution_add_fusion
  382.7 0.2 reduce-scatter.3.cloned.1.call-start
  383.0 4.5 fusion.5
  387.4 4.1 fusion.1
  391.6 2.3 copy.11
  393.9 3.8 fusion.2
  397.7 2.3 copy.12
  400.0 3.9 convolution_convert_fusion
  403.8 109.2 %reduce-scatter.5.cloned.1.call-done = f32[32,1024]{1,0:T(8,128)} async-done(((f32[1024,1024]{1,0:T(8,128)}), f32[32,1024]{1,0:T(8,128)}) %reduce-scatter.5.cloned.1.call-update) | async-done | bytes 131088 | tf_op jit(solution)/shard_map/reduce_scatter | solution.py:51
  513.0 1.5 convert_element_type.34
  514.6 128.7 %reduce-scatter.3.cloned.1.call-done = f32[32,1024]{1,0:T(8,128)} async-done(((f32[1024,1024]{1,0:T(8,128)}), f32[32,1024]{1,0:T(8,128)}) %reduce-scatter.3.cloned.1.call-update) | async-done | bytes 131088 | tf_op jit(solution)/shard_map/reduce_scatter | solution.py:32
  643.3 1.5 convert_element_type.31
  (16 shorter events, 0.2 us)
Async XLA Ops:
  7.2 95.0 %copy-start = (bf16[1024,512]{1,0:T(8,128)(2,1)S(1)}, bf16[1024,512]{1,0:T(8,128)(2,1)}, u32[]{:S(2)}) copy-start(bf16[1024,512]{1,0:T(8,128)(2,1)} %param.6) | copy-start | bytes 3145732
  7.2 91.6 %all-gather.2.cloned.1.call-start = ((), (), s32[]{:S(2)}) async-start(), calls=%async_computation.3 | async-start | bytes 2162688 | tf_op jit(solution)/shard_map/all_gather | solution.py:20
  10.4 95.6 %all-to-all-start = ((bf16[32,32,1024]{2,1,0:T(8,128)(2,1)}), bf16[32,32,1024]{2,1,0:T(8,128)(2,1)S(1)}, u32[]{:S(2)}, u32[]{:S(2)}) async-start(bf16[32,32,1024]{2,1,0:T(8,128)(2,1)} %stack.2), calls=%async_computation.1 | async-start | bytes 4194304 | tf_op jit(solution)/shard_map/all_to_all | solution.py:39
  21.8 351.7 %all-reduce.3.cloned.1.call-start = ((), (), s32[]{:S(2)}) async-start(), calls=%async_computation.6 | async-start | bytes 12582912 | tf_op jit(solution)/shard_map/psum | solution.py:25
  98.8 3.3 copy-start.4
  105.9 4.6 copy-start.1
  110.5 402.5 %reduce-scatter.5.cloned.1.call-start = ((), (), s32[]{:S(2)}) async-start(), calls=%async_computation.5 | async-start | bytes 4325376 | tf_op jit(solution)/shard_map/reduce_scatter | solution.py:51
  377.8 1.3 copy-start.3
  377.8 1.6 copy-start.2
  382.7 260.6 %reduce-scatter.3.cloned.1.call-start = ((), (), s32[]{:S(2)}) async-start(), calls=%async_computation.4 | async-start | bytes 4325376 | tf_op jit(solution)/shard_map/reduce_scatter | solution.py:32
Sparse Core Ops, SparseCore 0:
  10.8 87.9 all-gather.1
  110.7 262.8 all-reduce.2
  382.8 130.1 reduce-scatter.4
  517.1 126.1 reduce-scatter.2
